TPU v7x, 32 devices: a whole 2x2x4 slice. The times are simulated.
32 devices in a mesh: mesh: 32 (over z, y, x, core).
Axes of the slice: x: 2, y: 2, z: 4, core: 2. Of those that a mesh axis runs over, the one named last changes fastest.
Arguments:
- states: float32 [196608, 256], P('mesh'), may hold values from -30 to 30
- inv_sqrt_mass: float32 [196608], P('mesh'), may hold values from 0.25 to 1.75
- element_blocks: bfloat16 [512, 512, 512], P('mesh'), may hold values from -0.25 to 0.25
- element_nodes: int32 [512, 512], P('mesh'), may hold values from 0 to 6143, as said below
- element_counts: int32 [32], P('mesh'), may hold values from 1 to 16, as said below
- node_counts: int32 [32], replicated, may hold values from 4608 to 6144, as said below
- boundary_rows: int32 [32, 2, 384], P('mesh'), may hold values from 0 to 4607, as said below
Outputs:
- rotated: float32 [196608, 256], P('mesh')
Inputs may be any that keep to these rules, and one draw needn't show every extreme that they name: `node_counts`: live node rows of each device; some device has 6144. `element_counts`: live element slots of each device (the first slots are live); some device has 16. `element_nodes`: every entry is below its device's node count. `boundary_rows`: for each device the 768 entries are distinct rows below 4608.
All inputs are finite; a program needn't handle non-finite values.
Results may differ from a plain program's by a relative error of at most 0.0077.
Values sent between devices are 32-bit elements; how exact they have to be, the bound alone decides.
A program may use at most 128 MiB of HBM per device.

v0:
```python
import jax
import jax.numpy as jnp
from jax import lax
from jax.sharding import PartitionSpec as P


def passed_along(block, axis, distance):
    devices = range(lax.axis_size(axis))
    route = [(i - distance, i) for i in devices if i - distance in devices]
    return lax.ppermute(block, axis, route)


def body(
    states, inv_sqrt_mass, element_blocks, element_nodes, element_counts, node_counts, boundary_rows
):
    position = lax.axis_index("mesh")
    devices = lax.axis_size("mesh")
    row_total = states.shape[0]
    width = states.shape[1]
    slots = element_blocks.shape[0]
    lower_rows = boundary_rows[0, 0]
    upper_rows = boundary_rows[0, 1]
    shared = lower_rows.shape[0]
    has_below = position >= 1
    owner_vals, owner_mass = passed_along(
        (states[upper_rows], inv_sqrt_mass[upper_rows]), "mesh", 1
    )
    field = states.at[lower_rows].set(jnp.where(has_below, owner_vals, states[lower_rows]))
    mass = inv_sqrt_mass.at[lower_rows].set(
        jnp.where(has_below, owner_mass, inv_sqrt_mass[lower_rows])
    )
    live_slots = element_counts[0]
    row_index = jnp.arange(row_total)
    slot_index = jnp.arange(slots)
    slot_live = slot_index < live_slots

    def ham(values):
        scaled = (mass[:, None] * values).astype(jnp.bfloat16)
        empty = jnp.zeros((row_total, width), jnp.float32)

        def add_element(slot, total):
            rows = element_nodes[slot]

            def compute(acc):
                part = jnp.dot(
                    element_blocks[slot], scaled[rows], preferred_element_type=jnp.float32
                )
                return acc.at[rows].add(part)

            return lax.cond(slot_live[slot], compute, lambda acc: acc, total)

        local = lax.fori_loop(0, slots, add_element, empty)
        coming_up = passed_along(local[upper_rows], "mesh", 1)
        coming_down = passed_along(local[lower_rows], "mesh", -1)
        assembled = local.at[lower_rows].add(coming_up).at[upper_rows].add(coming_down)
        return mass[:, None] * assembled

    center = 0.5
    half_width = 1.5
    first = (ham(field) - center * field) / half_width
    second = 2.0 * (ham(first) - center * first) / half_width - field
    filtered = 2.0 * (ham(second) - center * second) / half_width - first
    live = row_index < node_counts[position]
    in_lower = jnp.any(row_index[:, None] == lower_rows[None, :], axis=1)
    owned = live & jnp.logical_not(in_lower & has_below)
    weighted = jnp.where(owned[:, None], filtered, 0.0)
    partial_value = lax.dot_general(
        weighted,
        weighted,
        (((0,), (0,)), ((), ())),
        precision=lax.Precision.HIGHEST,
        preferred_element_type=jnp.float32,
    )
    gram = lax.psum(partial_value, "mesh")
    total = (jnp.sum(node_counts) - shared * (devices - 1)).astype(jnp.float32)
    gram = gram / total
    factor = jnp.linalg.cholesky(gram)
    inverse = jax.scipy.linalg.solve_triangular(
        factor, jnp.eye(width, dtype=jnp.float32), lower=True
    )
    rotated = jnp.dot(
        filtered, inverse.T, precision=lax.Precision.HIGHEST, preferred_element_type=jnp.float32
    )
    return jnp.where(live[:, None], rotated, 0.0)


def solution(mesh):
    in_specs = (
        P("mesh", None),
        P("mesh"),
        P("mesh", None, None),
        P("mesh", None),
        P("mesh"),
        P(),
        P("mesh", None, None),
    )
    out_specs = P("mesh", None)
    return jax.shard_map(body, mesh=mesh, in_specs=in_specs, out_specs=out_specs, check_vma=False)
```

profile of v0, /device:TPU:0, one launch (start us, length us, event | category | flops | bytes accessed | tf_op | source)
XLA Modules:
  0.0 1121.8 jit_solution(17529059180484307456)
XLA Ops:
  7.3 5.8 copy.66
  22.5 4.5 collective-permute-start.1
  33.3 9.7 scatter_custom_fusion.4
  49.4 61.7 %while.49 = (s32[]{:T(128)}, f32[6144,256]{1,0:T(8,128)}, pred[16]{0:T(512)(128)(4,1)S(1)}, s32[16,512]{1,0:T(8,128)}, bf16[16,512,512]{2,1,0:T(8,128)(2,1)}, /*index=5*/bf16[6144,256]{1,0:T(8,128)(2,1)S(1)}, s32[]{:T(128)}) while((s32[]{:T(128)}, f32[6144,256]{1,0:T(8,128)}, pred[16]{0:T(512)(128)(4,1)S(1)}, s32[16,512]{1,0:T(8,128)}, ...), condition=%wide.region_6.7_spmd, body=%wide.region_2.6_spmd.sunk | while | flops 134351360 | bytes 3422386 | solution.py:52
  50.7 13.8 %conditional.6 = (f32[6144,256]{1,0:T(8,128)}) conditional(s32[]{:T(128)} %bitcast.62, f32[6144,256]{1,0:T(8,128)} %get-tuple-element.664, (s32[16,512]{1,0:T(8,128)}, s32[]{:T(128)}, bf16[16,512,512]{2,1,0:T(8,128)(2,1)}, bf16[6144,256]{1,0:T(8,128)(2,1)S(1)}, f32[6144,256]{1,0:T(8,128)}) %tuple.128), branch_computations={%region_3.3_spmd, %region_4.5_spmd} | conditional | flops 134351360 | bytes 3422258 | solution.py:50
  55.5 8.9 scatter_fusion
  65.7 13.8 %conditional.6 = (f32[6144,256]{1,0:T(8,128)}) conditional(s32[]{:T(128)} %bitcast.62, f32[6144,256]{1,0:T(8,128)} %get-tuple-element.664, (s32[16,512]{1,0:T(8,128)}, s32[]{:T(128)}, bf16[16,512,512]{2,1,0:T(8,128)(2,1)}, bf16[6144,256]{1,0:T(8,128)(2,1)S(1)}, f32[6144,256]{1,0:T(8,128)}) %tuple.128), branch_computations={%region_3.3_spmd, %region_4.5_spmd} | conditional | flops 134351360 | bytes 3422258 | solution.py:50
  70.6 8.9 scatter_fusion
  80.7 13.8 %conditional.6 = (f32[6144,256]{1,0:T(8,128)}) conditional(s32[]{:T(128)} %bitcast.62, f32[6144,256]{1,0:T(8,128)} %get-tuple-element.664, (s32[16,512]{1,0:T(8,128)}, s32[]{:T(128)}, bf16[16,512,512]{2,1,0:T(8,128)(2,1)}, bf16[6144,256]{1,0:T(8,128)(2,1)S(1)}, f32[6144,256]{1,0:T(8,128)}) %tuple.128), branch_computations={%region_3.3_spmd, %region_4.5_spmd} | conditional | flops 134351360 | bytes 3422258 | solution.py:50
  85.6 8.9 scatter_fusion
  111.1 4.5 gather_fusion.6
  115.6 29.4 %collective-permute-start.2 = (f32[384,256]{1,0:T(8,128)S(1)}, f32[384,256]{1,0:T(8,128)S(1)}, u32[]{:S(2)}, u32[]{:S(2)}) collective-permute-start(f32[384,256]{1,0:T(8,128)S(1)} %gather_fusion.6), channel_id=1, source_target_pairs={{0,1},{1,2},{2,3},{3,4},{4,5},{5,6},{6,7},{7,8},{8,9},{9,10},{10,1... | collective-permute-start | bytes 1179656 | tf_op jit(solution)/shard_map/ppermute | solution.py:10
  145.0 4.5 gather_fusion.7
  151.2 7.8 scatter_fusion.4
  159.1 7.8 scatter_fusion.5
  166.9 5.8 multiply_convert_fusion.1
  175.8 61.7 %while.50 = (s32[]{:T(128)}, f32[6144,256]{1,0:T(8,128)}, pred[16]{0:T(512)(128)(4,1)S(1)}, s32[16,512]{1,0:T(8,128)}, bf16[16,512,512]{2,1,0:T(8,128)(2,1)}, /*index=5*/bf16[6144,256]{1,0:T(8,128)(2,1)S(1)}, s32[]{:T(128)}) while((s32[]{:T(128)}, f32[6144,256]{1,0:T(8,128)}, pred[16]{0:T(512)(128)(4,1)S(1)}, s32[16,512]{1,0:T(8,128)}, ...), condition=%wide.region_13.14_spmd, body=%wide.region_9.13_spmd.sunk | while | flops 134351360 | bytes 3422386 | solution.py:52
  177.0 13.8 %conditional.7 = (f32[6144,256]{1,0:T(8,128)}) conditional(s32[]{:T(128)} %bitcast.63, f32[6144,256]{1,0:T(8,128)} %get-tuple-element.685, (s32[16,512]{1,0:T(8,128)}, s32[]{:T(128)}, bf16[16,512,512]{2,1,0:T(8,128)(2,1)}, bf16[6144,256]{1,0:T(8,128)(2,1)S(1)}, f32[6144,256]{1,0:T(8,128)}) %tuple.130), branch_computations={%region_10.10_spmd, %region_11.12_spmd} | conditional | flops 134351360 | bytes 3422258 | solution.py:50
  181.9 8.9 scatter_fusion.1
  192.0 13.8 %conditional.7 = (f32[6144,256]{1,0:T(8,128)}) conditional(s32[]{:T(128)} %bitcast.63, f32[6144,256]{1,0:T(8,128)} %get-tuple-element.685, (s32[16,512]{1,0:T(8,128)}, s32[]{:T(128)}, bf16[16,512,512]{2,1,0:T(8,128)(2,1)}, bf16[6144,256]{1,0:T(8,128)(2,1)S(1)}, f32[6144,256]{1,0:T(8,128)}) %tuple.130), branch_computations={%region_10.10_spmd, %region_11.12_spmd} | conditional | flops 134351360 | bytes 3422258 | solution.py:50
  196.9 8.9 scatter_fusion.1
  207.0 13.8 %conditional.7 = (f32[6144,256]{1,0:T(8,128)}) conditional(s32[]{:T(128)} %bitcast.63, f32[6144,256]{1,0:T(8,128)} %get-tuple-element.685, (s32[16,512]{1,0:T(8,128)}, s32[]{:T(128)}, bf16[16,512,512]{2,1,0:T(8,128)(2,1)}, bf16[6144,256]{1,0:T(8,128)(2,1)S(1)}, f32[6144,256]{1,0:T(8,128)}) %tuple.130), branch_computations={%region_10.10_spmd, %region_11.12_spmd} | conditional | flops 134351360 | bytes 3422258 | solution.py:50
  211.9 8.9 scatter_fusion.1
  237.5 4.5 gather_fusion.8
  241.9 30.5 %collective-permute-start.4 = (f32[384,256]{1,0:T(8,128)S(1)}, f32[384,256]{1,0:T(8,128)S(1)}, u32[]{:S(2)}, u32[]{:S(2)}) collective-permute-start(f32[384,256]{1,0:T(8,128)S(1)} %gather_fusion.8), channel_id=1, source_target_pairs={{0,1},{1,2},{2,3},{3,4},{4,5},{5,6},{6,7},{7,8},{8,9},{9,10},{10,1... | collective-permute-start | bytes 1179656 | tf_op jit(solution)/shard_map/ppermute | solution.py:10
  278.2 8.0 scatter_fusion.6
  286.2 7.8 scatter_fusion.7
  294.1 7.5 multiply_convert_fusion
  304.7 61.8 %while.51 = (s32[]{:T(128)}, f32[6144,256]{1,0:T(8,128)}, pred[16]{0:T(512)(128)(4,1)S(1)}, s32[16,512]{1,0:T(8,128)}, bf16[16,512,512]{2,1,0:T(8,128)(2,1)}, /*index=5*/bf16[6144,256]{1,0:T(8,128)(2,1)S(1)}, s32[]{:T(128)}) while((s32[]{:T(128)}, f32[6144,256]{1,0:T(8,128)}, pred[16]{0:T(512)(128)(4,1)S(1)}, s32[16,512]{1,0:T(8,128)}, ...), condition=%wide.region_20.21_spmd, body=%wide.region_16.20_spmd.sunk | while | flops 134351360 | bytes 3422386 | solution.py:52
  305.9 13.8 %conditional.8 = (f32[6144,256]{1,0:T(8,128)}) conditional(s32[]{:T(128)} %bitcast.64, f32[6144,256]{1,0:T(8,128)} %get-tuple-element.706, (s32[16,512]{1,0:T(8,128)}, s32[]{:T(128)}, bf16[16,512,512]{2,1,0:T(8,128)(2,1)}, bf16[6144,256]{1,0:T(8,128)(2,1)S(1)}, f32[6144,256]{1,0:T(8,128)}) %tuple.132), branch_computations={%region_17.17_spmd, %region_18.19_spmd} | conditional | flops 134351360 | bytes 3422258 | solution.py:50
  310.8 9.0 scatter_fusion.2
  321.0 13.8 %conditional.8 = (f32[6144,256]{1,0:T(8,128)}) conditional(s32[]{:T(128)} %bitcast.64, f32[6144,256]{1,0:T(8,128)} %get-tuple-element.706, (s32[16,512]{1,0:T(8,128)}, s32[]{:T(128)}, bf16[16,512,512]{2,1,0:T(8,128)(2,1)}, bf16[6144,256]{1,0:T(8,128)(2,1)S(1)}, f32[6144,256]{1,0:T(8,128)}) %tuple.132), branch_computations={%region_17.17_spmd, %region_18.19_spmd} | conditional | flops 134351360 | bytes 3422258 | solution.py:50
  325.8 9.0 scatter_fusion.2
  336.0 13.8 %conditional.8 = (f32[6144,256]{1,0:T(8,128)}) conditional(s32[]{:T(128)} %bitcast.64, f32[6144,256]{1,0:T(8,128)} %get-tuple-element.706, (s32[16,512]{1,0:T(8,128)}, s32[]{:T(128)}, bf16[16,512,512]{2,1,0:T(8,128)(2,1)}, bf16[6144,256]{1,0:T(8,128)(2,1)S(1)}, f32[6144,256]{1,0:T(8,128)}) %tuple.132), branch_computations={%region_17.17_spmd, %region_18.19_spmd} | conditional | flops 134351360 | bytes 3422258 | solution.py:50
  340.9 9.0 scatter_fusion.2
  366.4 4.5 gather_fusion.10
  370.9 4.5 gather_fusion.11
  375.4 57.9 %collective-permute-start.6 = (f32[384,256]{1,0:T(8,128)S(1)}, f32[384,256]{1,0:T(8,128)S(1)}, u32[]{:S(2)}, u32[]{:S(2)}) collective-permute-start(f32[384,256]{1,0:T(8,128)S(1)} %gather_fusion.10), channel_id=1, source_target_pairs={{0,1},{1,2},{2,3},{3,4},{4,5},{5,6},{6,7},{7,8},{8,9},{9,10},{10,1... | collective-permute-start | bytes 1179656 | tf_op jit(solution)/shard_map/ppermute | solution.py:10
  437.4 7.9 scatter_fusion.8
  445.2 7.9 scatter_fusion.9
  453.1 9.7 multiply_subtract_fusion
  465.5 12.9 %fusion.13 = f32[256,256]{0,1:T(8,128)} fusion(f32[6144,256]{1,0:T(8,128)S(1)} %multiply_subtract_fusion, pred[6144]{0:T(1024)(128)(4,1)S(1)} %not_and_fusion), kind=kOutput, calls=%fused_computation.47 | convolution fusion | flops 4833411072 | bytes 6559744 | tf_op jit(solution)/shard_map/dot_general | solution.py:67
  479.7 563.2 %all-reduce.3.cloned.1.call-done = f32[256,256]{0,1:T(8,128)} async-done(((f32[256,256]{0,1:T(8,128)}), f32[256,256]{0,1:T(8,128)}) %all-reduce.3.cloned.1.call-update) | async-done | bytes 262160 | tf_op jit(solution)/shard_map/psum | solution.py:74
  1045.5 11.7 %cholesky.50 = f32[128,128]{1,0:T(8,128)S(1)} custom-call(f32[128,128]{1,0:T(8,128)S(1)} %cholesky.118), custom_call_target="Cholesky" | custom-call | tf_op jit(solution)/shard_map/jit(cholesky)/cholesky | solution.py:77
  1057.3 9.8 custom-call.15
  1067.5 11.7 %cholesky.105 = f32[128,128]{1,0:T(8,128)S(1)} custom-call(f32[128,128]{1,0:T(8,128)S(1)} %convolution_subtract_fusion.1), custom_call_target="Cholesky" | custom-call | tf_op jit(solution)/shard_map/jit(cholesky)/cholesky | solution.py:77
  1085.1 19.8 %custom-call.16 = f32[2,128,128]{1,2,0:T(8,128)S(1)} custom-call(f32[2,128,128]{2,1,0:T(8,128)S(1)} %get-tuple-element.459), custom_call_target="InvertDiagBlocksLowerTriangular" | custom-call | tf_op jit(solution)/shard_map/jit(_solve_triangular)/triangular_solve | solution.py:78
  1105.8 8.9 convolution_select_fusion
  (190 shorter events, 128.4 us)
Async XLA Ops:
  6.5 1036.4 %all-reduce.3.cloned.1.call-start = ((), (), s32[]{:S(2)}) async-start(), calls=%async_computation | async-start | bytes 524288 | tf_op jit(solution)/shard_map/psum | solution.py:74
  7.3 5.8 copy-start.1
  15.7 14.6 %collective-permute-start = (f32[384]{0:T(512)S(1)}, f32[384]{0:T(512)S(1)}, u32[]{:S(2)}, u32[]{:S(2)}) collective-permute-start(f32[384]{0:T(512)S(1)} %gather_fusion.3), channel_id=1, source_target_pairs={{0,1},{1,2},{2,3},{3,4},{4,5},{5,6},{6,7},{7,8},{8,9},{9,10},{10,1... | collective-permute-start | bytes 4616 | tf_op jit(solution)/shard_map/ppermute | solution.py:10
  22.5 10.8 collective-permute-start.1
  115.6 35.6 %collective-permute-start.2 = (f32[384,256]{1,0:T(8,128)S(1)}, f32[384,256]{1,0:T(8,128)S(1)}, u32[]{:S(2)}, u32[]{:S(2)}) collective-permute-start(f32[384,256]{1,0:T(8,128)S(1)} %gather_fusion.6), channel_id=1, source_target_pairs={{0,1},{1,2},{2,3},{3,4},{4,5},{5,6},{6,7},{7,8},{8,9},{9,10},{10,1... | collective-permute-start | bytes 1179656 | tf_op jit(solution)/shard_map/ppermute | solution.py:10
  149.4 9.6 collective-permute-start.3
  241.9 36.3 %collective-permute-start.4 = (f32[384,256]{1,0:T(8,128)S(1)}, f32[384,256]{1,0:T(8,128)S(1)}, u32[]{:S(2)}, u32[]{:S(2)}) collective-permute-start(f32[384,256]{1,0:T(8,128)S(1)} %gather_fusion.8), channel_id=1, source_target_pairs={{0,1},{1,2},{2,3},{3,4},{4,5},{5,6},{6,7},{7,8},{8,9},{9,10},{10,1... | collective-permute-start | bytes 1179656 | tf_op jit(solution)/shard_map/ppermute | solution.py:10
  276.9 9.3 collective-permute-start.5
  366.4 69.0 %copy-start.2 = (s32[32]{0:T(128)S(1)}, s32[32]{0:T(128)}, u32[]{:S(2)}) copy-start(s32[32]{0:T(128)} %param.24) | copy-start | bytes 388
  375.4 62.0 %collective-permute-start.6 = (f32[384,256]{1,0:T(8,128)S(1)}, f32[384,256]{1,0:T(8,128)S(1)}, u32[]{:S(2)}, u32[]{:S(2)}) collective-permute-start(f32[384,256]{1,0:T(8,128)S(1)} %gather_fusion.10), channel_id=1, source_target_pairs={{0,1},{1,2},{2,3},{3,4},{4,5},{5,6},{6,7},{7,8},{8,9},{9,10},{10,1... | collective-permute-start | bytes 1179656 | tf_op jit(solution)/shard_map/ppermute | solution.py:10
  433.3 12.0 %collective-permute-start.7 = (f32[384,256]{1,0:T(8,128)S(1)}, f32[384,256]{1,0:T(8,128)S(1)}, u32[]{:S(2)}, u32[]{:S(2)}) collective-permute-start(f32[384,256]{1,0:T(8,128)S(1)} %gather_fusion.11), channel_id=1, source_target_pairs={{1,0},{2,1},{3,2},{4,3},{5,4},{6,5},{7,6},{8,7},{9,8},{10,9},{11,1... | collective-permute-start | bytes 1179656 | tf_op jit(solution)/shard_map/ppermute | solution.py:10
  462.9 2.7 copy-start
Sparse Core Ops, SparseCore 0:
  478.5 564.3 all-reduce.2
where the time goes:
time: 1140 us; the launch traced here: 1120 us
  waiting for transfers between devices  563 us (49%)
  other arithmetic  229 us (20%)
  starting transfers between devices  129 us (11%)
  local copies, waits for them, and re-layouts  109 us (10%)
  matrix products  42.3 us (4%)
  loops' own time  32.5 us (3%)
  between operations  16.5 us (1%)
    psum x1, waiting for transfers between devices, body(): gram = lax.psum(partial_value, 'mesh')  563 us
    ppermute x8, starting transfers between devices, passed_along(): return lax.ppermute(block, axis, route)  129 us
    scatter-add x9, other arithmetic, compute(): return acc.at[rows].add(part)  80.4 us
    scatter-add x6, other arithmetic, ham(): local.at[lower_rows].add(coming_up).at[upper_rows].add(coming_down)  47.2 us
    another operation x6, other arithmetic, body(): factor = jnp.linalg.cholesky(gram)  34 us
    another operation x3, loops' own time, ham(): local = lax.fori_loop(0, slots, add_element, empty)  31.6 us
    dynamic_slice x48, local copies, waits for them, and re-layouts, add_element(): return lax.cond(slot_live[slot], compute, lambda acc: acc, total)  28.8 us
  transfers between devices with their start and end apart: 9, of which 1 were waited for; matrix products, arithmetic and copies ran while one was open for 4% of the time, Pallas kernels for 0%

commit v1 on v0

v1 whole, which is shorter than its diff:
```python
import functools

import jax
import jax.numpy as jnp
from jax import lax
from jax.experimental import pallas as pl
from jax.experimental.pallas import tpu as pltpu
from jax.sharding import PartitionSpec as P

CENTER = 0.5
HALF = 1.5
LANES = 128
BLK = 512
GROUP = 16
CHOL = 32


def passed_along(block, axis, distance):
    devices = range(lax.axis_size(axis))
    route = [(i - distance, i) for i in devices if i - distance in devices]
    return lax.ppermute(block, axis, route)


def pair(start):
    return pl.ds(pl.multiple_of(start, 2), 2)


def each_row(count, work, unroll=8):
    @pl.loop(0, count // unroll)
    def _(q):
        todo = [work(q * unroll + t) for t in range(unroll)]
        for stores in todo:
            for ref, index, value in stores:
                ref[index, :] = value


def gather_rows(out_ref, src_ref, rows_ref, count):
    each_row(count, lambda k: [(out_ref, pair(2 * k), src_ref[pair(rows_ref[k]), :])])


def element(e, nodes, dup, mats, scaled, acc, gbuf, gb16, pbuf):
    size = gb16.shape[0]
    base = e * size

    @pl.loop(0, size // 32)
    def _(q):
        for t in range(32):
            k = q * 32 + t
            gbuf[pair(2 * k), :] = scaled[pair(nodes[base + k]), :]

    gb16[:, :LANES] = gbuf[pl.ds(0, size, stride=2), :].astype(jnp.bfloat16)
    gb16[:, LANES:] = gbuf[pl.ds(1, size, stride=2), :].astype(jnp.bfloat16)
    for c in range(size // 128):
        part = jnp.dot(
            mats[0, c * 128 : (c + 1) * 128, :], gb16[...], preferred_element_type=jnp.float32
        )
        pbuf[pl.ds(c * 256, 128, stride=2), :] = part[:, :LANES]
        pbuf[pl.ds(c * 256 + 1, 128, stride=2), :] = part[:, LANES:]

    @pl.loop(0, size // GROUP)
    def _(q):
        first = q * GROUP
        flag = dup[e * (size // GROUP) + q]

        @pl.when(flag == 0)
        def _():
            rows = [nodes[base + first + t] for t in range(GROUP)]
            sums = [
                acc[pair(rows[t]), :] + pbuf[pair(2 * (first + t)), :] for t in range(GROUP)
            ]
            for t in range(GROUP):
                acc[pair(rows[t]), :] = sums[t]

        @pl.when(flag != 0)
        def _():
            for t in range(GROUP):
                row = nodes[base + first + t]
                acc[pair(row), :] = acc[pair(row), :] + pbuf[pair(2 * (first + t)), :]


def first_kernel(nb, nodes, dup, count, low, up, below, states, mass_in, rvals, rmass, mats,
                 x, mass, acc, send_up, send_low, mlow, mup, scaled, gbuf, gb16, pbuf):
    i = pl.program_id(0)
    shared = low.shape[0]

    @pl.when(i < nb)
    def _():
        block = pl.ds(pl.multiple_of(i * 2 * BLK, 2 * BLK), 2 * BLK)
        m = mass_in[...]
        mass[block, :] = m
        acc[block, :] = jnp.zeros_like(m)
        gbuf[pl.ds(0, BLK, stride=2), :] = states[:, :LANES]
        gbuf[pl.ds(1, BLK, stride=2), :] = states[:, LANES:]
        v = gbuf[...]
        x[block, :] = v
        scaled[block, :] = m * v

    @pl.when((i == nb - 1) & (below[0] != 0))
    def _():
        def fix(k):
            row, v, m = pair(low[k]), rvals[pair(2 * k), :], rmass[pair(2 * k), :]
            return [(x, row, v), (mass, row, m), (scaled, row, m * v)]

        each_row(shared, fix)

    @pl.when(i == nb - 1)
    def _():
        gather_rows(mlow, mass, low, shared)
        gather_rows(mup, mass, up, shared)

    @pl.when((i >= nb) & (i - nb < count[0]))
    def _():
        element(i - nb, nodes, dup, mats, scaled, acc, gbuf, gb16, pbuf)

    @pl.when(i == pl.num_programs(0) - 1)
    def _():
        gather_rows(send_up, acc, up, shared)
        gather_rows(send_low, acc, low, shared)


def assemble(stage, i, nb, low, up, old, mass_in, xa, xb, coming_up, coming_down, mlow, mup, x,
             scaled):
    shared = low.shape[0]
    gain = 1.0 / HALF if stage == 1 else 2.0 / HALF

    @pl.when(i < nb)
    def _():
        block = pl.ds(pl.multiple_of(i * 2 * BLK, 2 * BLK), 2 * BLK)
        m = mass_in[...]
        v = gain * (m * old[...] - CENTER * xa[...])
        if xb is not None:
            v = v - xb[...]
        x[block, :] = v
        if scaled is not None:
            scaled[block, :] = m * v

    @pl.when(i == nb - 1)
    def _():
        for rows, extra, masses in ((low, coming_up, mlow), (up, coming_down, mup)):
            def fix(k, rows=rows, extra=extra, masses=masses):
                row, here = pair(rows[k]), pair(2 * k)
                m = masses[here, :]
                v = x[row, :] + gain * (m * extra[here, :])
                stores = [(x, row, v)]
                if scaled is not None:
                    stores.append((scaled, row, m * v))
                return stores

            each_row(shared, fix)


def middle_kernel(stage, nb, nodes, dup, count, low, up, below, old, mass_in, xa, *refs):
    refs = list(refs)
    xb = refs.pop(0) if stage > 1 else None
    (coming_up, coming_down, mlow, mup, mats, x, acc, send_up, send_low, scaled, gbuf, gb16,
     pbuf) = refs
    i = pl.program_id(0)
    shared = low.shape[0]

    @pl.when(i < nb)
    def _():
        block = pl.ds(pl.multiple_of(i * 2 * BLK, 2 * BLK), 2 * BLK)
        acc[block, :] = jnp.zeros((2 * BLK, LANES), jnp.float32)

    assemble(stage, i, nb, low, up, old, mass_in, xa, xb, coming_up, coming_down, mlow, mup, x,
             scaled)

    @pl.when((i >= nb) & (i - nb < count[0]))
    def _():
        element(i - nb, nodes, dup, mats, scaled, acc, gbuf, gb16, pbuf)

    @pl.when(i == pl.num_programs(0) - 1)
    def _():
        gather_rows(send_up, acc, up, shared)
        gather_rows(send_low, acc, low, shared)


def split(v):
    high = v.astype(jnp.bfloat16)
    return high, (v - high.astype(jnp.float32)).astype(jnp.bfloat16)


def gram_kernel(nb, live, low, up, below, old, mass_in, xa, xb, coming_up, coming_down, mlow, mup,
                x, gram, kept, cross):
    i = pl.program_id(0)
    shared = low.shape[0]
    assemble(3, i, nb, low, up, old, mass_in, xa, xb, coming_up, coming_down, mlow, mup, x, None)

    @pl.when(i == nb - 1)
    def _():
        gram[...] = jnp.zeros_like(gram)
        cross[...] = jnp.zeros_like(cross)

    @pl.when((i == nb - 1) & (below[0] != 0))
    def _():
        gather_rows(kept, x, low, shared)
        zero = jnp.zeros((2, LANES), jnp.float32)
        each_row(shared, lambda k: [(x, pair(low[k]), zero)])

    @pl.when((i >= nb) & ((i - nb) * BLK < live[0]))
    def _():
        start = pl.multiple_of((i - nb) * 2 * BLK, 2 * BLK)
        v = jnp.concatenate(
            [x[pl.ds(start, BLK, stride=2), :], x[pl.ds(start + 1, BLK, stride=2), :]], axis=1
        )
        row = (i - nb) * BLK + lax.broadcasted_iota(jnp.int32, v.shape, 0)
        high, rest = split(jnp.where(row < live[0], v, 0.0))
        over_rows = (((0,), (0,)), ((), ()))
        gram[...] += lax.dot_general(high, high, over_rows, preferred_element_type=jnp.float32)
        cross[...] += lax.dot_general(high, rest, over_rows, preferred_element_type=jnp.float32)

    @pl.when((i == pl.num_programs(0) - 1) & (below[0] != 0))
    def _():
        each_row(shared, lambda k: [(x, pair(low[k]), kept[pair(2 * k), :])])

    @pl.when(i == pl.num_programs(0) - 1)
    def _():
        gram[...] += cross[...] + cross[...].T


def invert(mat):
    width = mat.shape[0]
    lane = lax.broadcasted_iota(jnp.int32, (CHOL, width), 1)
    sub = lax.broadcasted_iota(jnp.int32, (CHOL, width), 0)

    @pl.loop(0, width // CHOL)
    def _(k):
        first = pl.multiple_of(k * CHOL, CHOL)
        rows = pltpu.roll(mat[pl.ds(first, CHOL), :], width - first, 1)
        for j in range(CHOL):
            inv = lax.rsqrt(rows[j : j + 1, j : j + 1])
            col = rows[:, j : j + 1] * inv
            pivot = jnp.where(lane[:1] == j, 1.0, rows[j : j + 1, :]) * inv
            kept = jnp.where(lane == j, 0.0, rows)
            rows = jnp.where(sub > j, kept - col * pivot, jnp.where(sub == j, pivot, rows))
        rows = jnp.where((lane > sub) & (lane < CHOL), 0.0, rows)
        rows = pltpu.roll(rows, first, 1)
        mat[pl.ds(first, CHOL), :] = rows
        upper = jnp.where(lane >= first + CHOL, rows, 0.0)
        update = lax.dot_general(
            upper, rows, (((0,), (0,)), ((), ())), precision=lax.Precision.HIGHEST,
            preferred_element_type=jnp.float32,
        )
        r = lax.broadcasted_iota(jnp.int32, (width, width), 0)
        c = lax.broadcasted_iota(jnp.int32, (width, width), 1)
        old = jnp.where((r >= first + CHOL) & (c >= first) & (c < first + CHOL), 0.0, mat[...])
        mat[...] = old - update

    r = lax.broadcasted_iota(jnp.int32, (width, width), 0)
    c = lax.broadcasted_iota(jnp.int32, (width, width), 1)
    mat[...] = jnp.where(c <= r, mat[...], 0.0)


def rotate_kernel(live, gram, x, out, mat, high_w, rest_w):
    i = pl.program_id(0)

    @pl.when(i == 0)
    def _():
        mat[...] = gram[...]
        invert(mat)
        high, rest = split(mat[...].T)
        high_w[...] = high
        rest_w[...] = rest

    v = jnp.concatenate([x[pl.ds(0, BLK, stride=2), :], x[pl.ds(1, BLK, stride=2), :]], axis=1)
    high, rest = split(v)
    dot = functools.partial(jnp.dot, preferred_element_type=jnp.float32)
    turned = dot(high, high_w[...]) + dot(rest, high_w[...]) + dot(high, rest_w[...])
    row = i * BLK + lax.broadcasted_iota(jnp.int32, v.shape, 0)
    out[...] = jnp.where(row < live[0], turned, 0.0)


def body(
    states, inv_sqrt_mass, element_blocks, element_nodes, element_counts, node_counts, boundary_rows
):
    position = lax.axis_index("mesh")
    devices = lax.axis_size("mesh")
    total_rows, width = states.shape
    slots, size = element_nodes.shape
    shared = boundary_rows.shape[2]
    nb = total_rows // BLK
    f32 = jnp.float32
    lower_rows, upper_rows = boundary_rows[0, 0], boundary_rows[0, 1]
    low, up = 2 * lower_rows, 2 * upper_rows
    below = (position >= 1).astype(jnp.int32).reshape(1)
    live = node_counts[position].reshape(1)
    nodes = (2 * element_nodes).reshape(slots * size)
    groups = element_nodes.reshape(slots * size // GROUP, GROUP)
    same = (groups[:, :, None] == groups[:, None, :]) & (
        jnp.arange(GROUP)[:, None] < jnp.arange(GROUP)[None, :]
    )
    dup = jnp.any(same, axis=(1, 2)).astype(jnp.int32)
    mass2 = jnp.broadcast_to(inv_sqrt_mass[:, None, None], (total_rows, 2, LANES)).reshape(
        2 * total_rows, LANES
    )

    owner_vals, owner_mass = passed_along(
        (states[upper_rows], inv_sqrt_mass[upper_rows]), "mesh", 1
    )
    rvals = owner_vals.reshape(2 * shared, LANES)
    rmass = jnp.broadcast_to(owner_mass[:, None, None], (shared, 2, LANES)).reshape(
        2 * shared, LANES
    )

    rows_shape = jax.ShapeDtypeStruct((2 * total_rows, LANES), f32)
    edge_shape = jax.ShapeDtypeStruct((2 * shared, LANES), f32)
    whole = pl.BlockSpec((2 * total_rows, LANES), lambda i, *_: (0, 0))
    edge = pl.BlockSpec((2 * shared, LANES), lambda i, *_: (0, 0))
    part = pl.BlockSpec((2 * BLK, LANES), lambda i, *_: (jnp.minimum(i, nb - 1), 0))
    mats = pl.BlockSpec(
        (1, size, size),
        lambda i, nodes, dup, count, *_: (jnp.clip(i - nb, 0, count[0] - 1), 0, 0),
    )
    scratch = [
        pltpu.VMEM((2 * total_rows, LANES), f32),
        pltpu.VMEM((2 * size, LANES), f32),
        pltpu.VMEM((size, width), jnp.bfloat16),
        pltpu.VMEM((2 * size, LANES), f32),
    ]
    params = pltpu.CompilerParams(
        dimension_semantics=("arbitrary",), vmem_limit_bytes=60 * 1024 * 1024
    )
    scalars = (nodes, dup, element_counts, low, up, below)

    x0, mass, local, send_up, send_low, mlow, mup = pl.pallas_call(
        functools.partial(first_kernel, nb),
        out_shape=(rows_shape,) * 3 + (edge_shape,) * 4,
        grid_spec=pltpu.PrefetchScalarGridSpec(
            num_scalar_prefetch=6,
            grid=(nb + slots,),
            in_specs=[
                pl.BlockSpec((BLK, width), lambda i, *_: (jnp.minimum(i, nb - 1), 0)),
                part, edge, edge, mats,
            ],
            out_specs=[whole] * 3 + [edge] * 4,
            scratch_shapes=scratch,
        ),
        compiler_params=params,
        name="first",
    )(*scalars, states, mass2, rvals, rmass, element_blocks)

    def exchange():
        return passed_along(send_up, "mesh", 1), passed_along(send_low, "mesh", -1)

    fields = [x0]
    for stage in (1, 2):
        coming_up, coming_down = exchange()
        before = fields[-2:][::-1]
        x, local, send_up, send_low = pl.pallas_call(
            functools.partial(middle_kernel, stage, nb),
            out_shape=(rows_shape,) * 2 + (edge_shape,) * 2,
            grid_spec=pltpu.PrefetchScalarGridSpec(
                num_scalar_prefetch=6,
                grid=(nb + slots,),
                in_specs=[part] * (2 + len(before)) + [edge] * 4 + [mats],
                out_specs=[whole] * 2 + [edge] * 2,
                scratch_shapes=scratch,
            ),
            compiler_params=params,
            name="stage" + str(stage),
        )(*scalars, local, mass, *before, coming_up, coming_down, mlow, mup, element_blocks)
        fields.append(x)

    coming_up, coming_down = exchange()
    square = pl.BlockSpec((width, width), lambda i, *_: (0, 0))
    filtered, partial_value = pl.pallas_call(
        functools.partial(gram_kernel, nb),
        out_shape=(rows_shape, jax.ShapeDtypeStruct((width, width), f32)),
        grid_spec=pltpu.PrefetchScalarGridSpec(
            num_scalar_prefetch=4,
            grid=(2 * nb,),
            in_specs=[part] * 4 + [edge] * 4,
            out_specs=[whole, square],
            scratch_shapes=[
                pltpu.VMEM((2 * shared, LANES), f32),
                pltpu.VMEM((width, width), f32),
            ],
        ),
        compiler_params=params,
        name="gram",
    )(live, low, up, below, local, mass, fields[2], fields[1], coming_up, coming_down, mlow, mup)
    gram = lax.psum(partial_value, "mesh")
    total = (jnp.sum(node_counts) - shared * (devices - 1)).astype(f32)
    gram = gram / total
    return pl.pallas_call(
        rotate_kernel,
        out_shape=jax.ShapeDtypeStruct((total_rows, width), f32),
        grid_spec=pltpu.PrefetchScalarGridSpec(
            num_scalar_prefetch=1,
            grid=(nb,),
            in_specs=[square, pl.BlockSpec((2 * BLK, LANES), lambda i, *_: (i, 0))],
            out_specs=pl.BlockSpec((BLK, width), lambda i, *_: (i, 0)),
            scratch_shapes=[
                pltpu.VMEM((width, width), f32),
                pltpu.VMEM((width, width), jnp.bfloat16),
                pltpu.VMEM((width, width), jnp.bfloat16),
            ],
        ),
        compiler_params=params,
        name="rotate",
    )(live, gram, filtered)


def solution(mesh):
    in_specs = (
        P("mesh", None),
        P("mesh"),
        P("mesh", None, None),
        P("mesh", None),
        P("mesh"),
        P(),
        P("mesh", None, None),
    )
    out_specs = P("mesh", None)
    return jax.shard_map(body, mesh=mesh, in_specs=in_specs, out_specs=out_specs, check_vma=False)
```

time: 1140 us -> 461 us (0.40); the launches traced: 1120 us -> 460 us
  waiting for transfers between devices: 563 us -> 144 us
  other arithmetic: 229 us -> 4.43 us
  Pallas kernels: 0 us -> 156 us
  local copies, waits for them, and re-layouts: 109 us -> 22.6 us
  matrix products: 42.3 us -> 0 us
  loops' own time: 32.5 us -> 0 us
    psum x1, waiting for transfers between devices: 563 us -> 138 us  [body(): gram = lax.psum(partial_value, 'mesh')]
    pallas_call x0 -> x5, Pallas kernels: none -> 156 us  [the longest x2 64.6 us: body(): pl.pallas_call(functools.partial(middle_kernel, stage, nb), out_shape=(ro...]
    scatter-add x15 -> x0, other arithmetic: 128 us -> none  [the longest x9 80.4 us: compute(): return acc.at[rows].add(part)]
    another operation x9 -> x0, other arithmetic: 53.8 us -> none  [the longest x6 34 us: body(): factor = jnp.linalg.cholesky(gram)]
    gather x16 -> x0, local copies, waits for them, and re-layouts: 46.8 us -> none  [the longest x9 17.6 us: compute(): scaled[rows]]
    dot_general x11 -> x0, matrix products: 40.9 us -> none  [the longest x9 19.2 us: compute(): jnp.dot(element_blocks[slot], scaled[rows], preferred_element_type=jnp.fl...]
    another operation x52 -> x0, loops' own time: 32.5 us -> none  [the longest x3 31.6 us: ham(): local = lax.fori_loop(0, slots, add_element, empty)]
    dynamic_slice x49 -> x1, local copies, waits for them, and re-layouts: 29.4 us -> 0.67 us  [body(): live = node_counts[position].reshape(1)]
  transfers between devices with their start and end apart: 9 -> 9, of which waited for: 1 -> 6; matrix products, arithmetic and copies ran while one was open for 4% -> 2% of each run, Pallas kernels for 0% -> 0%
where the time goes in v1:
time: 461 us; the launch traced here: 460 us
  Pallas kernels  156 us (34%)
  waiting for transfers between devices  144 us (31%)
  starting transfers between devices  118 us (26%)
  local copies, waits for them, and re-layouts  22.6 us (5%)
  between operations  14.9 us (3%)
    psum x1, waiting for transfers between devices, body(): gram = lax.psum(partial_value, 'mesh')  138 us
    ppermute x8, starting transfers between devices, passed_along(): return lax.ppermute(block, axis, route)  118 us
    pallas_call x2, Pallas kernels, body(): pl.pallas_call(functools.partial(middle_kernel, stage, nb), out_shape=(ro...  64.6 us
    pallas_call x1, Pallas kernels, body(): pl.pallas_call(rotate_kernel, out_shape=jax.ShapeDtypeStruct((total_rows,...  37.4 us
    pallas_call x1, Pallas kernels, body(): pl.pallas_call(functools.partial(first_kernel, nb), out_shape=(rows_shape...  32.2 us
    pallas_call x1, Pallas kernels, body(): pl.pallas_call(functools.partial(gram_kernel, nb), out_shape=(rows_shape,...  22 us
  transfers between devices with their start and end apart: 9, of which 6 were waited for; matrix products, arithmetic and copies ran while one was open for 2% of the time, Pallas kernels for 0%

profile of v1, /device:TPU:0, one launch (start us, length us, event | category | flops | bytes accessed | tf_op | source)
XLA Modules:
  0.0 460.1 jit_solution(13473854515276737797)
XLA Ops:
  6.5 0.0 all-reduce.2.cloned.1.call-start
  6.5 0.8 fusion
  7.3 5.0 %gather_fusion = f32[384,256]{1,0:T(8,128)} fusion(f32[6144,256]{1,0:T(8,128)} %states.1, s32[1024]{0:T(1024)S(1)} %pad_clamp_fusion), kind=kCustom, calls=%fused_computation | custom fusion | bytes 787968 | tf_op jit(solution)/shard_map/gather | solution.py:298
  12.3 3.1 collective-permute-start
  15.4 3.4 gather_fusion.1
  18.8 3.8 collective-permute-start.1
  22.6 0.9 eq.15
  23.5 0.1 copy.8
  23.6 0.1 and_reduce_fusion
  23.8 0.0 copy-done.8
  23.8 0.6 multiply_reduce_fusion
  24.4 0.6 convert_element_type.7.dup
  25.0 0.6 copy.10
  26.3 0.0 copy-done
  26.3 0.9 broadcast_in_dim.12
  27.1 2.1 broadcast_in_dim.26
  29.2 0.0 collective-permute-done.1
  29.2 0.1 broadcast_in_dim.28
  29.4 0.1 broadcast_in_dim.29
  29.5 0.0 collective-permute-done
  29.5 1.8 reshape.66.rvals
  31.3 0.9 broadcast_in_dim.30.rmass
  32.2 3.7 broadcast_in_dim.27.mass_in
  36.0 32.2 %first.1 = (f32[12288,128]{1,0:T(8,128)}, f32[12288,128]{1,0:T(8,128)}, f32[12288,128]{1,0:T(8,128)}, f32[768,128]{1,0:T(8,128)}, f32[768,128]{1,0:T(8,128)}, /*index=5*/f32[768,128]{1,0:T(8,128)}, f32[768,128]{1,0:T(8,128)}) custom-call(s32[8192]{0:T(1024)} %bitcast.6, s32[512]{0:T(512)} %convert_element_type.7.dup, s32[1]{0:T(128)S(6)} %copy.12.count, ...), custom_call_target="tpu_custom_call" | custom-call | tf_op jit(solution)/shard_map/first/pallas_call | solution.py:325
  68.1 32.4 %collective-permute-start.2 = (f32[768,128]{1,0:T(8,128)}, f32[768,128]{1,0:T(8,128)S(1)}, u32[]{:S(2)}, u32[]{:S(2)}) collective-permute-start(f32[768,128]{1,0:T(8,128)} %get-tuple-element.25), channel_id=1, source_target_pairs={{0,1},{1,2},{2,3},{3,4},{4,5},{5,6},{6,7},{7,8},{8,9},{9,10},{10,1... | collective-permute-start | bytes 1179656 | tf_op jit(solution)/shard_map/ppermute | solution.py:21
  100.6 1.3 collective-permute-start.3
  101.9 0.2 collective-permute-done.2.refs_0_
  102.1 2.3 collective-permute-done.3.refs_1_
  104.4 0.7 copy-done.4
  105.1 31.6 %stage1.1 = (f32[12288,128]{1,0:T(8,128)}, f32[12288,128]{1,0:T(8,128)}, f32[768,128]{1,0:T(8,128)}, f32[768,128]{1,0:T(8,128)}) custom-call(s32[8192]{0:T(1024)} %bitcast.7, s32[512]{0:T(512)} %convert_element_type.7.dup, s32[1]{0:T(128)S(6)} %copy.12.count, s32[384]{0:T(512)} %get-tuple-element.40.low, s32[384]{0:T(512)} %get-tuple-element.39.up, ...), custom_call_target="tpu_custom_call" | custom-call | tf_op jit(solution)/shard_map/stage1/pallas_call | solution.py:349
  136.7 37.2 %collective-permute-start.4 = (f32[768,128]{1,0:T(8,128)}, f32[768,128]{1,0:T(8,128)S(1)}, u32[]{:S(2)}, u32[]{:S(2)}) collective-permute-start(f32[768,128]{1,0:T(8,128)} %get-tuple-element.31), channel_id=1, source_target_pairs={{0,1},{1,2},{2,3},{3,4},{4,5},{5,6},{6,7},{7,8},{8,9},{9,10},{10,1... | collective-permute-start | bytes 1179656 | tf_op jit(solution)/shard_map/ppermute | solution.py:21
  173.9 1.3 collective-permute-start.5
  175.2 0.2 collective-permute-done.4.refs_1_
  175.4 2.3 collective-permute-done.5.refs_2_
  177.7 0.7 copy-done.2
  178.5 33.1 %stage2.1 = (f32[12288,128]{1,0:T(8,128)}, f32[12288,128]{1,0:T(8,128)}, f32[768,128]{1,0:T(8,128)}, f32[768,128]{1,0:T(8,128)}) custom-call(s32[8192]{0:T(1024)} %bitcast.8, s32[512]{0:T(512)} %convert_element_type.7.dup, s32[1]{0:T(128)S(6)} %copy.12.count, s32[384]{0:T(512)} %get-tuple-element.40.low, s32[384]{0:T(512)} %get-tuple-element.39.up, ...), custom_call_target="tpu_custom_call" | custom-call | tf_op jit(solution)/shard_map/stage2/pallas_call | solution.py:349
  211.6 37.1 %collective-permute-start.6 = (f32[768,128]{1,0:T(8,128)}, f32[768,128]{1,0:T(8,128)S(1)}, u32[]{:S(2)}, u32[]{:S(2)}) collective-permute-start(f32[768,128]{1,0:T(8,128)} %get-tuple-element.35), channel_id=1, source_target_pairs={{0,1},{1,2},{2,3},{3,4},{4,5},{5,6},{6,7},{7,8},{8,9},{9,10},{10,1... | collective-permute-start | bytes 1179656 | tf_op jit(solution)/shard_map/ppermute | solution.py:21
  248.7 1.3 collective-permute-start.7
  250.0 0.7 dynamic_slice.3.live
  250.7 0.0 collective-permute-done.6.coming_up
  250.7 1.8 collective-permute-done.7.coming_down
  252.6 0.8 copy-done.6
  253.4 22.0 %gram.1 = (f32[12288,128]{1,0:T(8,128)}, f32[256,256]{1,0:T(8,128)}) custom-call(s32[1]{0:T(128)} %dynamic_slice.3.live, s32[384]{0:T(512)} %get-tuple-element.40.low, s32[384]{0:T(512)} %get-tuple-element.39.up, s32[1]{0:T(128)} %bitcast.below, f32[12288,128]{1,0:T(8,128)} %get-tuple-element.33.old, f32[12288,128]{1,0:T(8,128)} %get-tuple-element.23.mass_in, ...), custom_call_target="tpu_custom_call" | custom-call | tf_op jit(solution)/shard_map/gram/pallas_call | solution.py:366
  275.3 0.0 all-reduce.2.cloned.1.call-update
  275.4 0.6 reduce_sum.9
  276.7 137.6 %all-reduce.2.cloned.1.call-done = f32[256,256]{1,0:T(8,128)} async-done(((f32[256,256]{1,0:T(8,128)}), f32[256,256]{1,0:T(8,128)}) %all-reduce.2.cloned.1.call-update) | async-done | bytes 262160 | tf_op jit(solution)/shard_map/psum | solution.py:382
  414.2 1.7 broadcast_divide_fusion.gram
  415.9 37.4 %rotate.1 = f32[6144,256]{1,0:T(8,128)} custom-call(s32[1]{0:T(128)} %dynamic_slice.3.live, f32[256,256]{1,0:T(8,128)} %broadcast_divide_fusion.gram, f32[12288,128]{1,0:T(8,128)} %get-tuple-element.38.x), custom_call_target="tpu_custom_call" | custom-call | tf_op jit(solution)/shard_map/rotate/pallas_call | solution.py:385
  (18 shorter events, 0.0 us)
Async XLA Ops:
  6.5 17.2 %copy-start.8 = (s32[1,2,384]{2,1,0:T(2,128)S(1)}, s32[1,2,384]{2,1,0:T(2,128)}, u32[]{:S(2)}) copy-start(s32[1,2,384]{2,1,0:T(2,128)} %param.13) | copy-start | bytes 9220
  6.5 19.7 %copy-start = (f32[6144]{0:T(1024)S(1)}, f32[6144]{0:T(1024)}, u32[]{:S(2)}) copy-start(f32[6144]{0:T(1024)} %param.8) | copy-start | bytes 73732
  6.5 17.2 %copy-start.7 = (s32[16,512]{1,0:T(8,128)S(1)}, s32[16,512]{1,0:T(8,128)}, u32[]{:S(2)}) copy-start(s32[16,512]{1,0:T(8,128)} %param.10) | copy-start | bytes 98308
  6.5 407.7 %all-reduce.2.cloned.1.call-start = ((), (), s32[]{:S(2)}) async-start(), calls=%async_computation | async-start | bytes 524288 | tf_op jit(solution)/shard_map/psum | solution.py:382
  12.3 17.2 %collective-permute-start = (f32[384,256]{1,0:T(8,128)}, f32[384,256]{1,0:T(8,128)}, u32[]{:S(2)}, u32[]{:S(2)}) collective-permute-start(f32[384,256]{1,0:T(8,128)} %gather_fusion), channel_id=1, source_target_pairs={{0,1},{1,2},{2,3},{3,4},{4,5},{5,6},{6,7},{7,8},{8,9},{9,10},{10,1... | collective-permute-start | bytes 1179656 | tf_op jit(solution)/shard_map/ppermute | solution.py:21
  18.8 10.4 %collective-permute-start.1 = (f32[384]{0:T(512)S(1)}, f32[384]{0:T(512)S(1)}, u32[]{:S(2)}, u32[]{:S(2)}) collective-permute-start(f32[384]{0:T(512)S(1)} %gather_fusion.1), channel_id=1, source_target_pairs={{0,1},{1,2},{2,3},{3,4},{4,5},{5,6},{6,7},{7,8},{8,9},{9,10},{10,1... | collective-permute-start | bytes 4616 | tf_op jit(solution)/shard_map/ppermute | solution.py:21
  68.1 34.0 %collective-permute-start.2 = (f32[768,128]{1,0:T(8,128)}, f32[768,128]{1,0:T(8,128)S(1)}, u32[]{:S(2)}, u32[]{:S(2)}) collective-permute-start(f32[768,128]{1,0:T(8,128)} %get-tuple-element.25), channel_id=1, source_target_pairs={{0,1},{1,2},{2,3},{3,4},{4,5},{5,6},{6,7},{7,8},{8,9},{9,10},{10,1... | collective-permute-start | bytes 1179656 | tf_op jit(solution)/shard_map/ppermute | solution.py:21
  100.6 3.8 collective-permute-start.3
  102.1 2.3 copy-start.3
  104.4 0.7 copy-start.4
  136.7 38.7 %collective-permute-start.4 = (f32[768,128]{1,0:T(8,128)}, f32[768,128]{1,0:T(8,128)S(1)}, u32[]{:S(2)}, u32[]{:S(2)}) collective-permute-start(f32[768,128]{1,0:T(8,128)} %get-tuple-element.31), channel_id=1, source_target_pairs={{0,1},{1,2},{2,3},{3,4},{4,5},{5,6},{6,7},{7,8},{8,9},{9,10},{10,1... | collective-permute-start | bytes 1179656 | tf_op jit(solution)/shard_map/ppermute | solution.py:21
  173.9 3.8 collective-permute-start.5
  175.4 2.3 copy-start.1
  177.7 0.7 copy-start.2
  178.5 71.5 %copy-start.9 = (s32[32]{0:T(128)S(1)}, s32[32]{0:T(128)}, u32[]{:S(2)}) copy-start(s32[32]{0:T(128)} %param.12) | copy-start | bytes 388
  211.6 39.1 %collective-permute-start.6 = (f32[768,128]{1,0:T(8,128)}, f32[768,128]{1,0:T(8,128)S(1)}, u32[]{:S(2)}, u32[]{:S(2)}) collective-permute-start(f32[768,128]{1,0:T(8,128)} %get-tuple-element.35), channel_id=1, source_target_pairs={{0,1},{1,2},{2,3},{3,4},{4,5},{5,6},{6,7},{7,8},{8,9},{9,10},{10,1... | collective-permute-start | bytes 1179656 | tf_op jit(solution)/shard_map/ppermute | solution.py:21
  248.7 3.8 collective-permute-start.7
  250.7 1.8 copy-start.5
  252.5 0.8 copy-start.6
Sparse Core Ops, SparseCore 0:
  275.5 138.6 all-reduce.1
